TPU v7x, 128 devices: a whole 4x4x4 slice. The times are simulated.
128 devices in a mesh: row: 32 (over z, y, core), col: 4 (over x).
Axes of the slice: x: 4, y: 4, z: 4, core: 2. Of those that a mesh axis runs over, the one named last changes fastest.
Arguments:
- tokens: bfloat16 [16384, 2048], P('row', 'col'), may hold values from -6 to 6
- cotangent: bfloat16 [16384, 2048], P('row', 'col'), may hold values from -6 to 6
- destination: int32 [16384], P('row'), may hold values from 0 to 16383, as said below
- segment_ids: int32 [16384], P('row'), may hold values from 0 to 7, as said below
- attn_gain: float32 [2048], replicated, may hold values from 0.5 to 1.5
- w_query: bfloat16 [2048, 2048], P('row', 'col'), may hold values from -0.125 to 0.125
- w_key: bfloat16 [2048, 256], P('row', 'col'), may hold values from -0.125 to 0.125
- w_value: bfloat16 [2048, 256], P('row', 'col'), may hold values from -0.125 to 0.125
- w_output: bfloat16 [2048, 2048], P('row', 'col'), may hold values from -0.5 to 0.5
- ffn_gain: float32 [2048], replicated, may hold values from 0.5 to 1.5
- w_gate: bfloat16 [2048, 5632], P('row', 'col'), may hold values from -0.125 to 0.125
- w_up: bfloat16 [2048, 5632], P('row', 'col'), may hold values from -0.125 to 0.125
- w_down: bfloat16 [2048, 5632], P('row', 'col'), may hold values from -0.078125 to 0.078125
Outputs:
- output: bfloat16 [16384, 2048], P('row', 'col')
- input_grad: bfloat16 [16384, 2048], P('row', 'col')
- attn_gain_grad: float32 [2048], P('row')
- w_query_grad: float32 [2048, 2048], P('row', 'col')
- w_key_grad: float32 [2048, 256], P('row', 'col')
- w_value_grad: float32 [2048, 256], P('row', 'col')
- w_output_grad: float32 [2048, 2048], P('row', 'col')
- ffn_gain_grad: float32 [2048], P('row')
- w_gate_grad: float32 [2048, 5632], P('row', 'col')
- w_up_grad: float32 [2048, 5632], P('row', 'col')
- w_down_grad: float32 [2048, 5632], P('row', 'col')
Inputs may be any that keep to these rules, and one draw needn't show every extreme that they name: `destination`: A permutation; the tokens of each aligned block of 512 arriving tokens go to exactly 16 places in each aligned block of 512 balanced places. `segment_ids`: within each aligned block of 512 places the ids start at 0 and rise by one where a new sequence begins, so a block holds at most 8 sequences; in every draw some block holds a single sequence of 512 tokens and some block holds 8 sequences.
All inputs are finite; a program needn't handle non-finite values.
Results may differ from a plain program's by a relative error of at most 0.028.
Values may be sent and summed in bfloat16 or wider, within the bound.
No kernel may reach another device: no remote copies, remote signals or barrier semaphores. Data moves between devices by JAX's collectives and lax.ppermute only.
A program may use at most 128 MiB of HBM per device.

v0:
```python
from functools import partial
import jax
import jax.numpy as jnp
from jax import lax
from jax.sharding import PartitionSpec as P

HEADS = 32
KV = 4
HD = 64
EPS = 1e-05
ROPE_BASE = 10000.0


def rope_tables(positions):
    half_width = HD // 2
    freqs = ROPE_BASE ** (-(jnp.arange(half_width, dtype=jnp.float32) * 2.0 / HD))
    angles = positions.astype(jnp.float32)[:, None] * freqs[None, :]
    return (jnp.cos(angles)[:, None, :], jnp.sin(angles)[:, None, :])


def rotate(values, cosine, sine):
    half_width = values.shape[-1] // 2
    first = values[..., :half_width]
    second = values[..., half_width:]
    return jnp.concatenate(
        [first * cosine - second * sine, second * cosine + first * sine], axis=-1
    )


def rotate_back(grads, cosine, sine):
    half_width = grads.shape[-1] // 2
    first = grads[..., :half_width]
    second = grads[..., half_width:]
    return jnp.concatenate(
        [first * cosine + second * sine, second * cosine - first * sine], axis=-1
    )


def positions_of(segment_ids):
    index = jnp.arange(segment_ids.shape[0], dtype=jnp.int32)
    change = jnp.concatenate([jnp.ones((1,), dtype=jnp.bool_), segment_ids[1:] != segment_ids[:-1]])
    starts = jnp.where(change, index, jnp.zeros_like(index))
    return index - lax.cummax(starts, axis=0)


def allowed_pairs(segment_ids):
    index = jnp.arange(segment_ids.shape[0], dtype=jnp.int32)
    return (segment_ids[:, None] == segment_ids[None, :]) & (index[None, :] <= index[:, None])


def rms_scale(values):
    return lax.rsqrt(jnp.mean(values * values, axis=-1, keepdims=True) + EPS)


def norm_back(values, inv_root, gain, grads):
    normed = values * inv_root
    scaled = grads * gain
    result = inv_root * (scaled - normed * jnp.mean(scaled * normed, axis=-1, keepdims=True))
    return (result, jnp.sum(grads * normed, axis=0))


def matmul(left, right):
    return jnp.dot(left, right, preferred_element_type=jnp.float32)


def head_scores(query_head, key_head, allowed, scale_factor):
    scores = matmul(query_head, key_head.T) * scale_factor
    return jnp.where(allowed, scores, -1e30)


def head_forward(inputs, key_heads, value_heads, allowed, scale_factor):
    query_head, kv_slot = inputs
    scores = head_scores(query_head, key_heads[kv_slot], allowed, scale_factor)
    peak = jnp.max(scores, axis=-1, keepdims=True)
    expo = jnp.exp(scores - peak)
    total = jnp.sum(expo, axis=-1, keepdims=True)
    probs = expo / total
    mixed = matmul(probs.astype(jnp.bfloat16), value_heads[kv_slot])
    return (mixed, (peak + jnp.log(total))[:, 0])


def head_backward(inputs, key_heads, value_heads, allowed, scale_factor):
    query_head, kv_slot, grad_head, log_total = inputs
    key_head = key_heads[kv_slot]
    value_head = value_heads[kv_slot]
    scores = head_scores(query_head, key_head, allowed, scale_factor)
    probs = jnp.exp(scores - log_total[:, None])
    prob_grad = matmul(grad_head, value_head.T)
    value_grad = matmul(probs.astype(jnp.bfloat16).T, grad_head)
    inner = jnp.sum(probs * prob_grad, axis=-1, keepdims=True)
    score_grad = (probs * (prob_grad - inner)).astype(jnp.bfloat16)
    query_grad = matmul(score_grad, key_head) * scale_factor
    key_grad = matmul(score_grad.T, query_head) * scale_factor
    return (query_grad, key_grad, value_grad)


def body(
    tokens,
    cotangent,
    destination,
    segment_ids,
    attn_gain,
    w_query,
    w_key,
    w_value,
    w_output,
    ffn_gain,
    w_gate,
    w_up,
    w_down,
):
    row_count = tokens.shape[0]
    quarter = tokens.shape[1]
    col_start = lax.axis_index("col") * quarter
    group_size = HEADS // KV
    send_order = jnp.argsort(destination)
    slot_ids = destination[send_order] % row_count
    arrived_rows, arrived_grads, arrived_slots = (
        lax.all_to_all(tokens[send_order], "row", split_axis=0, concat_axis=0, tiled=True),
        lax.all_to_all(cotangent[send_order], "row", split_axis=0, concat_axis=0, tiled=True),
        lax.all_to_all(slot_ids, "row", split_axis=0, concat_axis=0, tiled=True),
    )
    placing = jnp.argsort(arrived_slots)
    full_rows, full_grads = (
        lax.all_gather(arrived_rows[placing], "col", axis=1, tiled=True),
        lax.all_gather(arrived_grads[placing], "col", axis=1, tiled=True),
    )
    query_w, key_w, value_w, output_w = (
        lax.all_gather(w_query, "row", axis=0, tiled=True),
        lax.all_gather(w_key, "row", axis=0, tiled=True),
        lax.all_gather(w_value, "row", axis=0, tiled=True),
        lax.all_gather(w_output, "row", axis=0, tiled=True),
    )
    cosine, sine = rope_tables(positions_of(segment_ids))
    allowed = allowed_pairs(segment_ids)
    rows_wide = full_rows.astype(jnp.float32)
    inv_one = rms_scale(rows_wide)
    normed_one = (rows_wide * inv_one * attn_gain).astype(jnp.bfloat16)
    query = matmul(normed_one, query_w)
    key_raw = matmul(normed_one, key_w)
    value_raw = matmul(normed_one, value_w)
    query_heads_count = query.shape[1] // HD
    kv_count = key_raw.shape[1] // HD
    query_rot = (
        rotate(query.reshape(row_count, query_heads_count, HD), cosine, sine)
        .astype(jnp.bfloat16)
        .transpose(1, 0, 2)
    )
    key_rot = (
        rotate(key_raw.reshape(row_count, kv_count, HD), cosine, sine)
        .astype(jnp.bfloat16)
        .transpose(1, 0, 2)
    )
    value_heads = value_raw.astype(jnp.bfloat16).reshape(row_count, kv_count, HD).transpose(1, 0, 2)
    kv_slots = jnp.arange(query_heads_count, dtype=jnp.int32) // group_size
    scale_factor = HD ** (-0.5)
    mixed_heads, log_totals = lax.map(
        partial(
            head_forward,
            key_heads=key_rot,
            value_heads=value_heads,
            allowed=allowed,
            scale_factor=scale_factor,
        ),
        (query_rot, kv_slots),
    )
    mixed = (
        mixed_heads.transpose(1, 0, 2)
        .reshape(row_count, query_heads_count * HD)
        .astype(jnp.bfloat16)
    )
    attn_terms = matmul(mixed, output_w.T)
    attn_full = lax.psum(attn_terms, "col")
    resid = rows_wide + attn_full
    inv_two = rms_scale(resid)
    normed_two = (resid * inv_two * ffn_gain).astype(jnp.bfloat16)
    resid_part = lax.dynamic_slice_in_dim(resid, col_start, quarter, 1)
    gate_w, up_w, down_w = (
        lax.all_gather(w_gate, "row", axis=0, tiled=True),
        lax.all_gather(w_up, "row", axis=0, tiled=True),
        lax.all_gather(w_down, "row", axis=0, tiled=True),
    )
    gate = matmul(normed_two, gate_w)
    upper = matmul(normed_two, up_w)
    sigmoid_gate = jax.nn.sigmoid(gate)
    activ = (gate * sigmoid_gate * upper).astype(jnp.bfloat16)
    ffn_share = lax.psum_scatter(
        matmul(activ, down_w.T).astype(jnp.bfloat16), "col", scatter_dimension=1, tiled=True
    ).astype(jnp.float32)
    output_share = (resid_part + ffn_share).astype(jnp.bfloat16)
    gate_w, up_w, down_w = (
        lax.all_gather(w_gate, "row", axis=0, tiled=True),
        lax.all_gather(w_up, "row", axis=0, tiled=True),
        lax.all_gather(w_down, "row", axis=0, tiled=True),
    )
    down_weight_grad = matmul(full_grads.T, activ)
    act_grad = matmul(full_grads, down_w)
    gate_grad = (act_grad * upper * sigmoid_gate * (1.0 + gate * (1.0 - sigmoid_gate))).astype(
        jnp.bfloat16
    )
    up_grad = (act_grad * gate * sigmoid_gate).astype(jnp.bfloat16)
    gate_weight_grad = matmul(normed_two.T, gate_grad)
    up_weight_grad = matmul(normed_two.T, up_grad)
    normed_terms_two = matmul(gate_grad, gate_w.T) + matmul(up_grad, up_w.T)
    normed_grad_two = lax.psum(normed_terms_two, "col")
    resid_norm_grad, ffn_gain_grad = norm_back(resid, inv_two, ffn_gain, normed_grad_two)
    resid_grad = full_grads.astype(jnp.float32) + resid_norm_grad
    attn_grad_low = resid_grad.astype(jnp.bfloat16)
    ffn_results = (
        lax.psum_scatter(
            gate_weight_grad.astype(jnp.bfloat16), "row", scatter_dimension=0, tiled=True
        ).astype(jnp.float32),
        lax.psum_scatter(
            up_weight_grad.astype(jnp.bfloat16), "row", scatter_dimension=0, tiled=True
        ).astype(jnp.float32),
        lax.psum_scatter(
            down_weight_grad.astype(jnp.bfloat16), "row", scatter_dimension=0, tiled=True
        ).astype(jnp.float32),
        lax.psum_scatter(
            ffn_gain_grad.astype(jnp.bfloat16), "row", scatter_dimension=0, tiled=True
        ).astype(jnp.float32),
    )
    query_w, key_w, value_w, output_w = (
        lax.all_gather(w_query, "row", axis=0, tiled=True),
        lax.all_gather(w_key, "row", axis=0, tiled=True),
        lax.all_gather(w_value, "row", axis=0, tiled=True),
        lax.all_gather(w_output, "row", axis=0, tiled=True),
    )
    output_weight_grad = matmul(attn_grad_low.T, mixed)
    mixed_grad = matmul(attn_grad_low, output_w).astype(jnp.bfloat16)
    mixed_grad_heads = mixed_grad.reshape(row_count, query_heads_count, HD).transpose(1, 0, 2)
    query_grads, key_grads, value_grads = lax.map(
        partial(
            head_backward,
            key_heads=key_rot,
            value_heads=value_heads,
            allowed=allowed,
            scale_factor=scale_factor,
        ),
        (query_rot, kv_slots, mixed_grad_heads, log_totals),
    )
    query_grad = (
        rotate_back(query_grads.transpose(1, 0, 2), cosine, sine)
        .reshape(row_count, query_heads_count * HD)
        .astype(jnp.bfloat16)
    )
    key_sum = key_grads.reshape(kv_count, group_size, row_count, HD).sum(axis=1).transpose(1, 0, 2)
    key_grad = (
        rotate_back(key_sum, cosine, sine).reshape(row_count, kv_count * HD).astype(jnp.bfloat16)
    )
    value_sum = (
        value_grads.reshape(kv_count, group_size, row_count, HD).sum(axis=1).transpose(1, 0, 2)
    )
    value_grad = value_sum.reshape(row_count, kv_count * HD).astype(jnp.bfloat16)
    query_weight_grad = matmul(normed_one.T, query_grad)
    key_weight_grad = matmul(normed_one.T, key_grad)
    value_weight_grad = matmul(normed_one.T, value_grad)
    normed_terms_one = (
        matmul(query_grad, query_w.T) + matmul(key_grad, key_w.T) + matmul(value_grad, value_w.T)
    )
    normed_grad_one = lax.psum(normed_terms_one.astype(jnp.bfloat16), "col").astype(jnp.float32)
    rows_norm_grad, attn_gain_grad = norm_back(rows_wide, inv_one, attn_gain, normed_grad_one)
    rows_grad = resid_grad + rows_norm_grad
    input_share = lax.dynamic_slice_in_dim(rows_grad, col_start, quarter, 1).astype(jnp.bfloat16)
    attn_results = (
        lax.psum_scatter(
            query_weight_grad.astype(jnp.bfloat16), "row", scatter_dimension=0, tiled=True
        ).astype(jnp.float32),
        lax.psum_scatter(
            key_weight_grad.astype(jnp.bfloat16), "row", scatter_dimension=0, tiled=True
        ).astype(jnp.float32),
        lax.psum_scatter(
            value_weight_grad.astype(jnp.bfloat16), "row", scatter_dimension=0, tiled=True
        ).astype(jnp.float32),
        lax.psum_scatter(
            output_weight_grad.astype(jnp.bfloat16), "row", scatter_dimension=0, tiled=True
        ).astype(jnp.float32),
        lax.psum_scatter(
            attn_gain_grad.astype(jnp.bfloat16), "row", scatter_dimension=0, tiled=True
        ).astype(jnp.float32),
    )
    back_rows, back_grads = (
        lax.all_to_all(output_share[arrived_slots], "row", split_axis=0, concat_axis=0, tiled=True),
        lax.all_to_all(input_share[arrived_slots], "row", split_axis=0, concat_axis=0, tiled=True),
    )
    restore = jnp.argsort(send_order)
    return (
        back_rows[restore],
        back_grads[restore],
        attn_results[4],
        attn_results[0],
        attn_results[1],
        attn_results[2],
        attn_results[3],
        ffn_results[3],
        ffn_results[0],
        ffn_results[1],
        ffn_results[2],
    )


def solution(mesh):
    placed = (
        P("row", "col"),
        P("row", "col"),
        P("row"),
        P("row"),
        P(),
        P("row", "col"),
        P("row", "col"),
        P("row", "col"),
        P("row", "col"),
        P(),
        P("row", "col"),
        P("row", "col"),
        P("row", "col"),
    )
    return jax.shard_map(
        body,
        mesh=mesh,
        in_specs=placed,
        out_specs=(
            P("row", "col"),
            P("row", "col"),
            P("row"),
            P("row", "col"),
            P("row", "col"),
            P("row", "col"),
            P("row", "col"),
            P("row"),
            P("row", "col"),
            P("row", "col"),
            P("row", "col"),
        ),
        check_vma=False,
    )
```

profile of v0, /device:TPU:0, one launch (start us, length us, event | category | flops | bytes accessed | tf_op | source)
XLA Modules:
  0.0 1312.7 jit_solution(15525933860058886407)
XLA Ops:
  16.6 8.4 all-to-all-start.1
  53.0 22.4 %all_gather.36 = bf16[2048,64]{1,0:T(8,128)(2,1)S(1)} all-gather(bf16[64,64]{1,0:T(8,128)(2,1)S(1)} %copy-done.22), channel_id=1, replica_groups=mesh['row'=32,'col'=4] {'row'}, dimensions={0}, use_global_device_ids=true | all-gather | bytes 270336 | tf_op jit(solution)/shard_map/all_gather | solution.py:130
  75.5 26.7 %all_gather.37 = bf16[2048,64]{1,0:T(8,128)(2,1)} all-gather(bf16[64,64]{1,0:T(8,128)(2,1)S(1)} %copy-done.23), channel_id=1, replica_groups=mesh['row'=32,'col'=4] {'row'}, dimensions={0}, use_global_device_ids=true | all-gather | bytes 270336 | tf_op jit(solution)/shard_map/all_gather | solution.py:131
  111.2 14.4 %all-gather.10.cloned.1.call-done = bf16[2048,512]{1,0:T(8,128)(2,1)} async-done(((bf16[64,512]{1,0:T(8,128)(2,1)}), bf16[2048,512]{1,0:T(8,128)(2,1)}) %all-gather.10.cloned.1.call-update) | async-done | bytes 2097168 | tf_op jit(solution)/shard_map/all_gather | solution.py:129
  129.4 24.0 %while.32 = (s32[]{:T(128)}, bf16[8,512,64]{1,2,0:T(8,128)(2,1)S(1)}, f32[8,512]{1,0:T(8,128)}, bf16[8,512,64]{2,1,0:T(8,128)(2,1)S(1)}, bf16[1,512,64]{2,1,0:T(...) while((s32[]{:T(128)}, bf16[8,512,64]{1,2,0:T(8,128)(2,1)S(1)}, ...), condition=%wide.region_8.9_spmd.clone.clone, body=%wide.region_5.8_spmd.clone.sunk.clone | while | flops 69991936 | bytes 3695189 | solution.py:157
  153.4 17.8 %all-gather.12.cloned.1.call-done = bf16[2048,512]{1,0:T(8,128)(2,1)} async-done(((bf16[64,512]{1,0:T(8,128)(2,1)}), bf16[2048,512]{1,0:T(8,128)(2,1)}) %all-gather.12.cloned.1.call-update) | async-done | bytes 2097168 | tf_op jit(solution)/shard_map/all_gather | solution.py:132
  180.0 17.1 %all_to_all.60 = bf16[32,16,512]{2,1,0:T(8,128)(2,1)S(1)} all-to-all(bf16[32,16,512]{2,1,0:T(8,128)(2,1)} %bitcast.194), channel_id=1, replica_groups=mesh['row'=32,'col'=4] {'row'}, dimensions={0} | all-to-all | bytes 1048576 | tf_op jit(solution)/shard_map/all_to_all | solution.py:120
  201.1 67.2 %all-reduce.7.cloned.1.call-done = f32[512,2048]{1,0:T(8,128)} async-done(((f32[512,2048]{1,0:T(8,128)}), f32[512,2048]{1,0:T(8,128)}) %all-reduce.7.cloned.1.call-update) | async-done | bytes 4194320 | tf_op jit(solution)/shard_map/psum | solution.py:173
  274.8 44.2 %all-gather.14.cloned.1.call-done = bf16[2048,1408]{1,0:T(8,128)(2,1)} async-done(((bf16[64,1408]{1,0:T(8,128)(2,1)}), bf16[2048,1408]{1,0:T(8,128)(2,1)}) %all-gather.14.cloned.1.call-update) | async-done | bytes 5767184 | tf_op jit(solution)/shard_map/all_gather | solution.py:179
  327.3 41.5 %all-gather.16.cloned.1.call-done = bf16[2048,1408]{1,0:T(8,128)(2,1)} async-done(((bf16[64,1408]{1,0:T(8,128)(2,1)}), bf16[2048,1408]{1,0:T(8,128)(2,1)}) %all-gather.16.cloned.1.call-update) | async-done | bytes 5767184 | tf_op jit(solution)/shard_map/all_gather | solution.py:180
  377.1 23.9 %all-gather.22.cloned.1.call-done = bf16[512,2048]{1,0:T(8,128)(2,1)} async-done(((bf16[512,512]{1,0:T(8,128)(2,1)}), bf16[512,2048]{1,0:T(8,128)(2,1)}) %all-gather.22.cloned.1.call-update) | async-done | bytes 2097168 | tf_op jit(solution)/shard_map/all_gather | solution.py:126
  400.9 51.0 %all-gather.18.cloned.1.call-done = bf16[2048,1408]{1,0:T(8,128)(2,1)} async-done(((bf16[64,1408]{1,0:T(8,128)(2,1)}), bf16[2048,1408]{1,0:T(8,128)(2,1)}) %all-gather.18.cloned.1.call-update) | async-done | bytes 5767184 | tf_op jit(solution)/shard_map/all_gather | solution.py:181
  452.0 10.3 multiply_convert_fusion.3
  482.2 83.7 %all-reduce.9.cloned.1.call-done = f32[512,2048]{1,0:T(8,128)} async-done(((f32[512,2048]{1,0:T(8,128)}), f32[512,2048]{1,0:T(8,128)}) %all-reduce.9.cloned.1.call-update) | async-done | bytes 4194320 | tf_op jit(solution)/shard_map/psum | solution.py:205
  579.3 65.5 %while.33 = (s32[]{:T(128)}, f32[8,512,64]{1,2,0:T(8,128)}, f32[8,512,64]{1,2,0:T(8,128)}, f32[8,512,64]{1,2,0:T(8,128)}, bf16[8,512,64]{2,1,0:T(8,128)(2,1)}, /...) while((s32[]{:T(128)}, f32[8,512,64]{1,2,0:T(8,128)}, ...), condition=%wide.region_17.18_spmd.clone.clone, body=%wide.region_15.17_spmd.clone.sunk.clone | while | flops 170982912 | bytes 8996457 | solution.py:232
  703.5 10.4 all-reduce.11.cloned.1.call-done
  733.4 61.5 %reduce-scatter.13.cloned.1.call-done = bf16[64,64]{1,0:T(8,128)(2,1)} async-done(((bf16[2048,64]{1,0:T(8,128)(2,1)}), bf16[64,64]{1,0:T(8,128)(2,1)}) %reduce-scatter.13.cloned.1.call-update) | async-done | bytes 8208 | tf_op jit(solution)/shard_map/reduce_scatter | solution.py:269
  796.2 78.5 %reduce-scatter.15.cloned.1.call-done = bf16[64,64]{1,0:T(8,128)(2,1)} async-done(((bf16[2048,64]{1,0:T(8,128)(2,1)}), bf16[64,64]{1,0:T(8,128)(2,1)}) %reduce-scatter.15.cloned.1.call-update) | async-done | bytes 8208 | tf_op jit(solution)/shard_map/reduce_scatter | solution.py:272
  878.7 64.4 %all-reduce.2 = (bf16[2048]{0:T(1024)(128)(2,1)S(1)}, bf16[2048]{0:T(1024)(128)(2,1)S(1)}) all-reduce(bf16[2048]{0:T(1024)(128)(2,1)S(1)} %get-tuple-element.249, bf16[2048]{0:T(1024)(128)(2,1)S(1)} %copy-done.20), channel_id=5, replica_groups=mesh['row'=32,'col'=4] {'row'}, use_global_device_ids=true, to_apply=%region_23.24.clone | all-reduce | flops 4096 | bytes 16384
  946.4 10.0 reduce-scatter.11.cloned.1.call-done
  957.9 80.2 %reduce-scatter.17.cloned.1.call-done = bf16[64,512]{1,0:T(8,128)(2,1)} async-done(((bf16[2048,512]{1,0:T(8,128)(2,1)}), bf16[64,512]{1,0:T(8,128)(2,1)}) %reduce-scatter.17.cloned.1.call-update) | async-done | bytes 65552 | tf_op jit(solution)/shard_map/reduce_scatter | solution.py:275
  1039.6 86.9 %reduce-scatter.19.cloned.1.call-done = bf16[64,1408]{1,0:T(8,128)(2,1)} async-done(((bf16[2048,1408]{1,0:T(8,128)(2,1)}), bf16[64,1408]{1,0:T(8,128)(2,1)}) %reduce-scatter.19.cloned.1.call-update) | async-done | bytes 180240 | tf_op jit(solution)/shard_map/reduce_scatter | solution.py:210
  1128.2 87.2 %reduce-scatter.21.cloned.1.call-done = bf16[64,1408]{1,0:T(8,128)(2,1)} async-done(((bf16[2048,1408]{1,0:T(8,128)(2,1)}), bf16[64,1408]{1,0:T(8,128)(2,1)}) %reduce-scatter.21.cloned.1.call-update) | async-done | bytes 180240 | tf_op jit(solution)/shard_map/reduce_scatter | solution.py:213
  1217.0 86.7 %reduce-scatter.23.cloned.1.call-done = bf16[64,1408]{1,0:T(8,128)(2,1)} async-done(((bf16[2048,1408]{1,0:T(8,128)(2,1)}), bf16[64,1408]{1,0:T(8,128)(2,1)}) %reduce-scatter.23.cloned.1.call-update) | async-done | bytes 180240 | tf_op jit(solution)/shard_map/reduce_scatter | solution.py:216
  (306 shorter events, 302.0 us)
Async XLA Ops:
  16.6 15.7 %all-to-all-start.1 = ((s32[32,16,1]{1,2,0:T(1,128)}), s32[32,16,1]{1,2,0:T(1,128)S(1)}, u32[]{:S(2)}, u32[]{:S(2)}) async-start(s32[32,16,1]{1,2,0:T(1,128)} %bitcast.2), calls=%async_computation.1 | async-start | bytes 32768 | tf_op jit(solution)/shard_map/all_to_all | solution.py:121
  32.3 15.7 %all-to-all-start = ((bf16[32,16,512]{2,1,0:T(8,128)(2,1)}), bf16[32,16,512]{2,1,0:T(8,128)(2,1)S(1)}, u32[]{:S(2)}, u32[]{:S(2)}) async-start(bf16[32,16,512]{2,1,0:T(8,128)(2,1)} %bitcast), calls=%async_computation | async-start | bytes 1048576 | tf_op jit(solution)/shard_map/all_to_all | solution.py:119
  36.2 66.3 %all-gather.20.cloned.1.call-start = ((), (), s32[]{:S(2)}) async-start(), calls=%async_computation.29 | async-start | bytes 2621440 | tf_op jit(solution)/shard_map/all_gather | solution.py:125
  50.6 75.0 %all-gather.10.cloned.1.call-start = ((), (), s32[]{:S(2)}) async-start(), calls=%async_computation.13 | async-start | bytes 2162688 | tf_op jit(solution)/shard_map/all_gather | solution.py:129
  51.4 119.8 %all-gather.12.cloned.1.call-start = ((), (), s32[]{:S(2)}) async-start(), calls=%async_computation.14 | async-start | bytes 2162688 | tf_op jit(solution)/shard_map/all_gather | solution.py:132
  52.1 216.2 %all-reduce.7.cloned.1.call-start = ((), (), s32[]{:S(2)}) async-start(), calls=%async_computation.15 | async-start | bytes 8388608 | tf_op jit(solution)/shard_map/psum | solution.py:173
  176.1 142.8 %all-gather.14.cloned.1.call-start = ((), (), s32[]{:S(2)}) async-start(), calls=%async_computation.16 | async-start | bytes 5947392 | tf_op jit(solution)/shard_map/all_gather | solution.py:179
  176.7 192.1 %all-gather.16.cloned.1.call-start = ((), (), s32[]{:S(2)}) async-start(), calls=%async_computation.17 | async-start | bytes 5947392 | tf_op jit(solution)/shard_map/all_gather | solution.py:180
  177.3 223.6 %all-gather.22.cloned.1.call-start = ((), (), s32[]{:S(2)}) async-start(), calls=%async_computation.30 | async-start | bytes 2621440 | tf_op jit(solution)/shard_map/all_gather | solution.py:126
  199.9 252.1 %all-gather.18.cloned.1.call-start = ((), (), s32[]{:S(2)}) async-start(), calls=%async_computation.18 | async-start | bytes 5947392 | tf_op jit(solution)/shard_map/all_gather | solution.py:181
  200.6 365.2 %all-reduce.9.cloned.1.call-start = ((), (), s32[]{:S(2)}) async-start(), calls=%async_computation.20 | async-start | bytes 8388608 | tf_op jit(solution)/shard_map/psum | solution.py:205
  474.0 218.0 %reduce-scatter.9.cloned.1.call-start = ((), (), s32[]{:S(2)}) async-start(), calls=%async_computation.19 | async-start | bytes 2621440 | tf_op jit(solution)/shard_map/reduce_scatter | solution.py:187
  482.1 231.8 %all-reduce.11.cloned.1.call-start = ((), (), s32[]{:S(2)}) async-start(), calls=%async_computation.21 | async-start | bytes 4194304 | tf_op jit(solution)/shard_map/psum | solution.py:261
  655.2 139.7 %reduce-scatter.13.cloned.1.call-start = ((), (), s32[]{:S(2)}) async-start(), calls=%async_computation.23 | async-start | bytes 540672 | tf_op jit(solution)/shard_map/reduce_scatter | solution.py:269
  657.1 217.6 %reduce-scatter.15.cloned.1.call-start = ((), (), s32[]{:S(2)}) async-start(), calls=%async_computation.24 | async-start | bytes 540672 | tf_op jit(solution)/shard_map/reduce_scatter | solution.py:272
  659.2 297.1 %reduce-scatter.11.cloned.1.call-start = ((), (), s32[]{:S(2)}) async-start(), calls=%async_computation.22 | async-start | bytes 2162688 | tf_op jit(solution)/shard_map/reduce_scatter | solution.py:266
  662.1 375.9 %reduce-scatter.17.cloned.1.call-start = ((), (), s32[]{:S(2)}) async-start(), calls=%async_computation.25 | async-start | bytes 2162688 | tf_op jit(solution)/shard_map/reduce_scatter | solution.py:275
  667.4 459.0 %reduce-scatter.19.cloned.1.call-start = ((), (), s32[]{:S(2)}) async-start(), calls=%async_computation.26 | async-start | bytes 5947392 | tf_op jit(solution)/shard_map/reduce_scatter | solution.py:210
  675.5 539.8 %reduce-scatter.21.cloned.1.call-start = ((), (), s32[]{:S(2)}) async-start(), calls=%async_computation.27 | async-start | bytes 5947392 | tf_op jit(solution)/shard_map/reduce_scatter | solution.py:213
  683.6 620.1 %reduce-scatter.23.cloned.1.call-start = ((), (), s32[]{:S(2)}) async-start(), calls=%async_computation.28 | async-start | bytes 5947392 | tf_op jit(solution)/shard_map/reduce_scatter | solution.py:216
  696.3 24.8 %all-to-all-start.2 = ((bf16[32,16,512]{2,1,0:T(8,128)(2,1)}), bf16[32,16,512]{2,1,0:T(8,128)(2,1)S(1)}, u32[]{:S(2)}, u32[]{:S(2)}) async-start(bf16[32,16,512]{2,1,0:T(8,128)(2,1)} %bitcast.14), calls=%async_computation.3 | async-start | bytes 1048576 | tf_op jit(solution)/shard_map/all_to_all | solution.py:283
  718.4 160.3 %copy-start.20 = (bf16[2048]{0:T(1024)(128)(2,1)S(1)}, bf16[2048]{0:T(1024)(128)(2,1)}, u32[]{:S(2)}) copy-start(bf16[2048]{0:T(1024)(128)(2,1)} %get-tuple-element.247) | copy-start | bytes 12292
  721.0 222.7 %all-to-all-start.4 = ((bf16[32,16,512]{2,1,0:T(8,128)(2,1)}), bf16[32,16,512]{2,1,0:T(8,128)(2,1)S(1)}, u32[]{:S(2)}, u32[]{:S(2)}) async-start(bf16[32,16,512]{2,1,0:T(8,128)(2,1)} %bitcast.24), calls=%async_computation.5 | async-start | bytes 1048576 | tf_op jit(solution)/shard_map/all_to_all | solution.py:284
  876.1 429.3 %copy-start.1 = (bf16[512,512]{1,0:T(8,128)(2,1)S(1)}, bf16[512,512]{1,0:T(8,128)(2,1)}, u32[]{:S(2)}) copy-start(bf16[512,512]{1,0:T(8,128)(2,1)} %param.17) | copy-start | bytes 1572868
  (32 other events, 623.6 us)
Sparse Core Ops, SparseCore 0:
  50.7 28.4 all-gather.19
  81.5 44.0 all-gather.9
  127.9 43.2 all-gather.11
  176.2 91.9 all-reduce.6
  270.6 48.3 all-gather.13
  321.3 47.4 all-gather.15
  371.1 29.7 all-gather.21
  403.4 48.4 all-gather.17
  474.1 91.7 all-reduce.8
  568.1 29.5 reduce-scatter.8
  655.3 58.5 all-reduce.10
  717.8 77.0 reduce-scatter.12
  798.4 76.3 reduce-scatter.14
  878.2 78.1 reduce-scatter.10
  959.8 78.2 reduce-scatter.16
  1041.7 84.7 reduce-scatter.18
  1130.5 84.7 reduce-scatter.20
  1218.9 84.7 reduce-scatter.22
where the time goes:
time: 1320 us; the launch traced here: 1310 us
  waiting for transfers between devices  860 us (65%)
  matrix products  170 us (13%)
  blocking collectives  131 us (10%)
  other arithmetic  55.9 us (4%)
  local copies, waits for them, and re-layouts  51.2 us (4%)
  starting transfers between devices  28.6 us (2%)
  between operations  16 us (1%)
    dot_general x77, matrix products, matmul(): return jnp.dot(left, right, preferred_element_type=jnp.float32)  170 us
    reduce_scatter x1, waiting for transfers between devices, body(): lax.psum_scatter(up_weight_grad.astype(jnp.bfloat16), 'row', scatter_dime...  87.2 us
    reduce_scatter x1, waiting for transfers between devices, body(): lax.psum_scatter(gate_weight_grad.astype(jnp.bfloat16), 'row', scatter_di...  86.9 us
    reduce_scatter x1, waiting for transfers between devices, body(): lax.psum_scatter(down_weight_grad.astype(jnp.bfloat16), 'row', scatter_di...  86.7 us
    psum x1, waiting for transfers between devices, body(): normed_grad_two = lax.psum(normed_terms_two, 'col')  83.7 us
    reduce_scatter x1, waiting for transfers between devices, body(): lax.psum_scatter(output_weight_grad.astype(jnp.bfloat16), 'row', scatter_...  80.2 us
    reduce_scatter x1, waiting for transfers between devices, body(): lax.psum_scatter(value_weight_grad.astype(jnp.bfloat16), 'row', scatter_d...  78.5 us
    psum x1, waiting for transfers between devices, body(): attn_full = lax.psum(attn_terms, 'col')  67.2 us
  transfers between devices with their start and end apart: 22, of which 18 were waited for; matrix products, arithmetic and copies ran while one was open for 18% of the time, Pallas kernels for 0%

commit v1 on v0

--- a/solution.py
+++ b/solution.py
@@ -170,7 +170,11 @@
         .astype(jnp.bfloat16)
     )
     attn_terms = matmul(mixed, output_w.T)
-    attn_full = lax.psum(attn_terms, "col")
+    attn_full = attn_terms
+    for hop in (1, 2):
+        attn_full = attn_full + lax.ppermute(
+            attn_full, "col", [(dev, dev ^ hop) for dev in range(4)]
+        )
     resid = rows_wide + attn_full
     inv_two = rms_scale(resid)
     normed_two = (resid * inv_two * ffn_gain).astype(jnp.bfloat16)

time: 1320 us -> 1270 us (0.962)
  waiting for transfers between devices: 860 us -> 803 us
    ppermute x0 -> x2, waiting for transfers between devices: none -> 191 us  [body(): lax.ppermute(attn_full, 'col', [(dev, dev ^ hop) for dev in range(4)])]
    psum x1 -> x0, waiting for transfers between devices: 67.2 us -> none  [body(): attn_full = lax.psum(attn_terms, 'col')]
    all_gather x1, waiting for transfers between devices: 51 us -> 0.01 us  [body(): lax.all_gather(w_down, 'row', axis=0, tiled=True)]
    all_gather x1, waiting for transfers between devices: 44.2 us -> 0.01 us  [body(): lax.all_gather(w_gate, 'row', axis=0, tiled=True)]
    all_gather x1, waiting for transfers between devices: 41.5 us -> 0.01 us  [body(): lax.all_gather(w_up, 'row', axis=0, tiled=True)]
    all_gather x1, waiting for transfers between devices: 23.9 us -> 0.01 us  [body(): lax.all_gather(arrived_grads[placing], 'col', axis=1, tiled=True)]
    all_gather x1, waiting for transfers between devices: 14.4 us -> 0.02 us  [body(): lax.all_gather(w_query, 'row', axis=0, tiled=True)]
  transfers between devices with their start and end apart: 22 -> 23, of which waited for: 18 -> 14; matrix products, arithmetic and copies ran while one was open for 18% -> 19% of each run, Pallas kernels for 0% -> 0%
where the time goes in v1:
time: 1270 us; the launch traced here: 1260 us
  waiting for transfers between devices  803 us (63%)
  matrix products  166 us (13%)
  blocking collectives  129 us (10%)
  other arithmetic  60.1 us (5%)
  local copies, waits for them, and re-layouts  50.5 us (4%)
  starting transfers between devices  33.1 us (3%)
  between operations  15.7 us (1%)
    ppermute x2, waiting for transfers between devices, body(): lax.ppermute(attn_full, 'col', [(dev, dev ^ hop) for dev in range(4)])  191 us
    dot_general x77, matrix products, matmul(): return jnp.dot(left, right, preferred_element_type=jnp.float32)  166 us
    reduce_scatter x1, waiting for transfers between devices, body(): lax.psum_scatter(gate_weight_grad.astype(jnp.bfloat16), 'row', scatter_di...  87.3 us
    reduce_scatter x1, waiting for transfers between devices, body(): lax.psum_scatter(down_weight_grad.astype(jnp.bfloat16), 'row', scatter_di...  87.1 us
    reduce_scatter x1, waiting for transfers between devices, body(): lax.psum_scatter(up_weight_grad.astype(jnp.bfloat16), 'row', scatter_dime...  86.7 us
    psum x1, waiting for transfers between devices, body(): normed_grad_two = lax.psum(normed_terms_two, 'col')  83.9 us
    reduce_scatter x1, waiting for transfers between devices, body(): lax.psum_scatter(output_weight_grad.astype(jnp.bfloat16), 'row', scatter_...  80.5 us
    reduce_scatter x1, waiting for transfers between devices, body(): lax.psum_scatter(value_weight_grad.astype(jnp.bfloat16), 'row', scatter_d...  78.8 us
  transfers between devices with their start and end apart: 23, of which 14 were waited for; matrix products, arithmetic and copies ran while one was open for 19% of the time, Pallas kernels for 0%

profile of v1, /device:TPU:0, one launch (start us, length us, event | category | flops | bytes accessed | tf_op | source)
XLA Modules:
  0.0 1256.8 jit_solution(2810117099235199229)
XLA Ops:
  16.6 8.4 all-to-all-start.1
  54.2 15.4 %all_to_all.60 = bf16[32,16,512]{2,1,0:T(8,128)(2,1)S(1)} all-to-all(bf16[32,16,512]{2,1,0:T(8,128)(2,1)S(1)} %bitcast.195), channel_id=1, replica_groups=mesh['row'=32,'col'=4] {'row'}, dimensions={0} | all-to-all | bytes 1048576 | tf_op jit(solution)/shard_map/all_to_all | solution.py:120
  75.0 22.4 %all_gather.36 = bf16[2048,64]{1,0:T(8,128)(2,1)S(1)} all-gather(bf16[64,64]{1,0:T(8,128)(2,1)S(1)} %copy-done.19), channel_id=1, replica_groups=mesh['row'=32,'col'=4] {'row'}, dimensions={0}, use_global_device_ids=true | all-gather | bytes 270336 | tf_op jit(solution)/shard_map/all_gather | solution.py:130
  97.4 26.7 %all_gather.37 = bf16[2048,64]{1,0:T(8,128)(2,1)} all-gather(bf16[64,64]{1,0:T(8,128)(2,1)S(1)} %copy-done.20), channel_id=1, replica_groups=mesh['row'=32,'col'=4] {'row'}, dimensions={0}, use_global_device_ids=true | all-gather | bytes 270336 | tf_op jit(solution)/shard_map/all_gather | solution.py:131
  136.9 24.1 %while.32 = (s32[]{:T(128)}, bf16[8,512,64]{1,2,0:T(8,128)(2,1)S(1)}, f32[8,512]{1,0:T(8,128)}, bf16[8,512,64]{2,1,0:T(8,128)(2,1)S(1)}, bf16[1,512,64]{2,1,0:T(...) while((s32[]{:T(128)}, bf16[8,512,64]{1,2,0:T(8,128)(2,1)S(1)}, ...), condition=%wide.region_8.9_spmd.clone.clone, body=%wide.region_5.8_spmd.clone.sunk.clone | while | flops 69991936 | bytes 3695189 | solution.py:157
  161.0 10.1 all-gather.12.cloned.1.call-done
  175.6 108.1 %collective-permute-done = f32[512,2048]{1,0:T(8,128)S(1)} collective-permute-done((f32[512,2048]{1,0:T(8,128)S(1)}, f32[512,2048]{1,0:T(8,128)S(1)}, u32[]{:S(2)}, u32[]{:S(2)}) %collective-permute-start) | collective-permute-done | bytes 4194336 | tf_op jit(solution)/shard_map/ppermute | solution.py:175
  289.8 8.3 fusion.77
  298.1 82.4 %collective-permute-done.1 = f32[512,2048]{1,0:T(8,128)} collective-permute-done((f32[512,2048]{1,0:T(8,128)}, f32[512,2048]{1,0:T(8,128)}, u32[]{:S(2)}, u32[]{:S(2)}) %collective-permute-start.1) | collective-permute-done | bytes 4194336 | tf_op jit(solution)/shard_map/ppermute | solution.py:175
  388.5 8.3 fusion.76
  396.8 10.7 multiply_convert_fusion.3
  424.5 83.9 %all-reduce.6.cloned.1.call-done = f32[512,2048]{1,0:T(8,128)} async-done(((f32[512,2048]{1,0:T(8,128)}), f32[512,2048]{1,0:T(8,128)}) %all-reduce.6.cloned.1.call-update) | async-done | bytes 4194320 | tf_op jit(solution)/shard_map/psum | solution.py:209
  521.8 65.5 %while.33 = (s32[]{:T(128)}, f32[8,512,64]{1,2,0:T(8,128)}, f32[8,512,64]{1,2,0:T(8,128)}, f32[8,512,64]{1,2,0:T(8,128)}, bf16[8,512,64]{2,1,0:T(8,128)(2,1)}, /...) while((s32[]{:T(128)}, f32[8,512,64]{1,2,0:T(8,128)}, ...), condition=%wide.region_16.17_spmd.clone.clone, body=%wide.region_14.16_spmd.clone.sunk.clone | while | flops 170982912 | bytes 8996457 | solution.py:236
  609.9 8.0 convolution_convert_fusion.2
  618.0 8.1 convolution_convert_fusion.1
  646.0 10.4 all-reduce.8.cloned.1.call-done
  675.9 62.0 %reduce-scatter.13.cloned.1.call-done = bf16[64,64]{1,0:T(8,128)(2,1)} async-done(((bf16[2048,64]{1,0:T(8,128)(2,1)}), bf16[64,64]{1,0:T(8,128)(2,1)}) %reduce-scatter.13.cloned.1.call-update) | async-done | bytes 8208 | tf_op jit(solution)/shard_map/reduce_scatter | solution.py:273
  739.2 78.8 %reduce-scatter.15.cloned.1.call-done = bf16[64,64]{1,0:T(8,128)(2,1)} async-done(((bf16[2048,64]{1,0:T(8,128)(2,1)}), bf16[64,64]{1,0:T(8,128)(2,1)}) %reduce-scatter.15.cloned.1.call-update) | async-done | bytes 8208 | tf_op jit(solution)/shard_map/reduce_scatter | solution.py:276
  822.0 64.1 %all-reduce.2 = (bf16[2048]{0:T(1024)(128)(2,1)S(1)}, bf16[2048]{0:T(1024)(128)(2,1)S(1)}) all-reduce(bf16[2048]{0:T(1024)(128)(2,1)S(1)} %get-tuple-element.249, bf16[2048]{0:T(1024)(128)(2,1)S(1)} %copy-done.18), channel_id=5, replica_groups=mesh['row'=32,'col'=4] {'row'}, use_global_device_ids=true, to_apply=%region_22.23.clone | all-reduce | flops 4096 | bytes 16384
  889.3 10.9 reduce-scatter.11.cloned.1.call-done
  901.7 80.5 %reduce-scatter.17.cloned.1.call-done = bf16[64,512]{1,0:T(8,128)(2,1)} async-done(((bf16[2048,512]{1,0:T(8,128)(2,1)}), bf16[64,512]{1,0:T(8,128)(2,1)}) %reduce-scatter.17.cloned.1.call-update) | async-done | bytes 65552 | tf_op jit(solution)/shard_map/reduce_scatter | solution.py:279
  983.7 87.3 %reduce-scatter.19.cloned.1.call-done = bf16[64,1408]{1,0:T(8,128)(2,1)} async-done(((bf16[2048,1408]{1,0:T(8,128)(2,1)}), bf16[64,1408]{1,0:T(8,128)(2,1)}) %reduce-scatter.19.cloned.1.call-update) | async-done | bytes 180240 | tf_op jit(solution)/shard_map/reduce_scatter | solution.py:214
  1072.7 86.7 %reduce-scatter.21.cloned.1.call-done = bf16[64,1408]{1,0:T(8,128)(2,1)} async-done(((bf16[2048,1408]{1,0:T(8,128)(2,1)}), bf16[64,1408]{1,0:T(8,128)(2,1)}) %reduce-scatter.21.cloned.1.call-update) | async-done | bytes 180240 | tf_op jit(solution)/shard_map/reduce_scatter | solution.py:217
  1161.0 87.1 %reduce-scatter.23.cloned.1.call-done = bf16[64,1408]{1,0:T(8,128)(2,1)} async-done(((bf16[2048,1408]{1,0:T(8,128)(2,1)}), bf16[64,1408]{1,0:T(8,128)(2,1)}) %reduce-scatter.23.cloned.1.call-update) | async-done | bytes 180240 | tf_op jit(solution)/shard_map/reduce_scatter | solution.py:220
  (304 shorter events, 272.1 us)
Async XLA Ops:
  16.6 15.7 %all-to-all-start.1 = ((s32[32,16,1]{1,2,0:T(1,128)}), s32[32,16,1]{1,2,0:T(1,128)S(1)}, u32[]{:S(2)}, u32[]{:S(2)}) async-start(s32[32,16,1]{1,2,0:T(1,128)} %bitcast.2), calls=%async_computation.1 | async-start | bytes 32768 | tf_op jit(solution)/shard_map/all_to_all | solution.py:121
  32.3 15.7 %all-to-all-start = ((bf16[32,16,512]{2,1,0:T(8,128)(2,1)}), bf16[32,16,512]{2,1,0:T(8,128)(2,1)S(1)}, u32[]{:S(2)}, u32[]{:S(2)}) async-start(bf16[32,16,512]{2,1,0:T(8,128)(2,1)} %bitcast), calls=%async_computation | async-start | bytes 1048576 | tf_op jit(solution)/shard_map/all_to_all | solution.py:119
  36.2 88.2 %all-gather.20.cloned.1.call-start = ((), (), s32[]{:S(2)}) async-start(), calls=%async_computation.28 | async-start | bytes 2621440 | tf_op jit(solution)/shard_map/all_gather | solution.py:125
  50.6 82.6 %all-gather.10.cloned.1.call-start = ((), (), s32[]{:S(2)}) async-start(), calls=%async_computation.13 | async-start | bytes 2162688 | tf_op jit(solution)/shard_map/all_gather | solution.py:129
  51.4 119.8 %all-gather.12.cloned.1.call-start = ((), (), s32[]{:S(2)}) async-start(), calls=%async_computation.14 | async-start | bytes 2162688 | tf_op jit(solution)/shard_map/all_gather | solution.py:132
  52.1 237.7 %all-gather.22.cloned.1.call-start = ((), (), s32[]{:S(2)}) async-start(), calls=%async_computation.29 | async-start | bytes 2621440 | tf_op jit(solution)/shard_map/all_gather | solution.py:126
  72.2 217.6 %all-gather.18.cloned.1.call-start = ((), (), s32[]{:S(2)}) async-start(), calls=%async_computation.17 | async-start | bytes 5947392 | tf_op jit(solution)/shard_map/all_gather | solution.py:185
  72.8 315.7 %all-gather.16.cloned.1.call-start = ((), (), s32[]{:S(2)}) async-start(), calls=%async_computation.16 | async-start | bytes 5947392 | tf_op jit(solution)/shard_map/all_gather | solution.py:184
  73.3 323.4 %all-gather.14.cloned.1.call-start = ((), (), s32[]{:S(2)}) async-start(), calls=%async_computation.15 | async-start | bytes 5947392 | tf_op jit(solution)/shard_map/all_gather | solution.py:183
  74.1 434.4 %all-reduce.6.cloned.1.call-start = ((), (), s32[]{:S(2)}) async-start(), calls=%async_computation.19 | async-start | bytes 8388608 | tf_op jit(solution)/shard_map/psum | solution.py:209
  174.0 109.7 %collective-permute-start = (f32[512,2048]{1,0:T(8,128)S(1)}, f32[512,2048]{1,0:T(8,128)S(1)}, u32[]{:S(2)}, u32[]{:S(2)}) collective-permute-start(f32[512,2048]{1,0:T(8,128)S(1)} %fusion.75), channel_id=1, source_target_pairs={{0,1},{1,0},{2,3},{3,2},{4,5},{5,4},{6,7},{7,6},{8,9},{9,8},{10,11... | collective-permute-start | bytes 12582920 | tf_op jit(solution)/shard_map/ppermute | solution.py:175
  286.4 94.1 %collective-permute-start.1 = (f32[512,2048]{1,0:T(8,128)}, f32[512,2048]{1,0:T(8,128)}, u32[]{:S(2)}, u32[]{:S(2)}) collective-permute-start(f32[512,2048]{1,0:T(8,128)} %add.162), channel_id=1, source_target_pairs={{0,2},{1,3},{2,0},{3,1},{4,6},{5,7},{6,4},{7,5},{8,10},{9,11},{10,... | collective-permute-start | bytes 12582920 | tf_op jit(solution)/shard_map/ppermute | solution.py:175
  416.3 218.2 %reduce-scatter.9.cloned.1.call-start = ((), (), s32[]{:S(2)}) async-start(), calls=%async_computation.18 | async-start | bytes 2621440 | tf_op jit(solution)/shard_map/reduce_scatter | solution.py:191
  424.5 232.0 %all-reduce.8.cloned.1.call-start = ((), (), s32[]{:S(2)}) async-start(), calls=%async_computation.20 | async-start | bytes 4194304 | tf_op jit(solution)/shard_map/psum | solution.py:265
  597.8 140.1 %reduce-scatter.13.cloned.1.call-start = ((), (), s32[]{:S(2)}) async-start(), calls=%async_computation.22 | async-start | bytes 540672 | tf_op jit(solution)/shard_map/reduce_scatter | solution.py:273
  599.7 218.3 %reduce-scatter.15.cloned.1.call-start = ((), (), s32[]{:S(2)}) async-start(), calls=%async_computation.23 | async-start | bytes 540672 | tf_op jit(solution)/shard_map/reduce_scatter | solution.py:276
  601.8 298.4 %reduce-scatter.11.cloned.1.call-start = ((), (), s32[]{:S(2)}) async-start(), calls=%async_computation.21 | async-start | bytes 2162688 | tf_op jit(solution)/shard_map/reduce_scatter | solution.py:270
  604.6 377.6 %reduce-scatter.17.cloned.1.call-start = ((), (), s32[]{:S(2)}) async-start(), calls=%async_computation.24 | async-start | bytes 2162688 | tf_op jit(solution)/shard_map/reduce_scatter | solution.py:279
  609.9 461.1 %reduce-scatter.19.cloned.1.call-start = ((), (), s32[]{:S(2)}) async-start(), calls=%async_computation.25 | async-start | bytes 5947392 | tf_op jit(solution)/shard_map/reduce_scatter | solution.py:214
  617.9 541.4 %reduce-scatter.21.cloned.1.call-start = ((), (), s32[]{:S(2)}) async-start(), calls=%async_computation.26 | async-start | bytes 5947392 | tf_op jit(solution)/shard_map/reduce_scatter | solution.py:217
  626.1 622.0 %reduce-scatter.23.cloned.1.call-start = ((), (), s32[]{:S(2)}) async-start(), calls=%async_computation.27 | async-start | bytes 5947392 | tf_op jit(solution)/shard_map/reduce_scatter | solution.py:220
  638.7 24.8 %all-to-all-start.2 = ((bf16[32,16,512]{2,1,0:T(8,128)(2,1)}), bf16[32,16,512]{2,1,0:T(8,128)(2,1)S(1)}, u32[]{:S(2)}, u32[]{:S(2)}) async-start(bf16[32,16,512]{2,1,0:T(8,128)(2,1)} %bitcast.194), calls=%async_computation.3 | async-start | bytes 1048576 | tf_op jit(solution)/shard_map/all_to_all | solution.py:287
  663.5 223.1 %all-to-all-start.4 = ((bf16[32,16,512]{2,1,0:T(8,128)(2,1)}), bf16[32,16,512]{2,1,0:T(8,128)(2,1)S(1)}, u32[]{:S(2)}, u32[]{:S(2)}) async-start(bf16[32,16,512]{2,1,0:T(8,128)(2,1)} %bitcast.24), calls=%async_computation.5 | async-start | bytes 1048576 | tf_op jit(solution)/shard_map/all_to_all | solution.py:288
  819.3 430.5 %copy-start.1 = (bf16[512,512]{1,0:T(8,128)(2,1)S(1)}, bf16[512,512]{1,0:T(8,128)(2,1)}, u32[]{:S(2)}) copy-start(bf16[512,512]{1,0:T(8,128)(2,1)} %param.17) | copy-start | bytes 1572868
  (31 other events, 771.9 us)
Sparse Core Ops, SparseCore 0:
  50.7 28.4 all-gather.19
  81.5 44.2 all-gather.9
  128.1 42.9 all-gather.11
  173.2 46.0 all-gather.21
  221.4 49.4 all-gather.17
  273.0 47.4 all-gather.15
  322.7 47.4 all-gather.13
  416.4 92.0 all-reduce.5
  511.0 29.4 reduce-scatter.8
  597.9 58.4 all-reduce.7
  660.8 77.0 reduce-scatter.12
  741.6 76.3 reduce-scatter.14
  822.0 78.1 reduce-scatter.10
  904.0 78.1 reduce-scatter.16
  986.3 84.7 reduce-scatter.18
  1074.6 84.6 reduce-scatter.20
  1163.4 84.6 reduce-scatter.22
